TPU v7x, 128 devices: a whole 4x4x4 slice. The times are simulated.
128 devices in a mesh: section: 2 (over z_lo), dp: 16 (over y, x), tensor: 4 (over z_hi, core).
Axes of the slice: x: 4, y: 4, z: 4 (z_hi: 2, z_lo: 2; z = z_hi * 2 + z_lo), core: 2. Of those that a mesh axis runs over, the one named last changes fastest.
Arguments:
- images: bfloat16 [48, 577, 768], P('dp', None, 'tensor'), may hold values from -6 to 6
- slot_table: int32 [32], P('dp'), may hold values from 0 to 3, as said below
- ln1_gain: float32 [2, 768], P('section'), may hold values from 0.5 to 1.5
- ln1_bias: float32 [2, 768], P('section'), may hold values from -1.5 to 1.5
- qkv_weight: bfloat16 [2, 768, 3, 768], P('section', None, None, 'tensor'), may hold values from -0.21875 to 0.21875
- qv_bias: float32 [2, 2, 768], P('section', None, 'tensor'), may hold values from -1.5 to 1.5
- out_weight: bfloat16 [2, 768, 768], P('section', 'tensor'), may hold values from -0.875 to 0.875
- out_bias: float32 [2, 768], P('section'), may hold values from -1.5 to 1.5
- ln2_gain: float32 [2, 768], P('section'), may hold values from 0.5 to 1.5
- ln2_bias: float32 [2, 768], P('section'), may hold values from -1.5 to 1.5
- fc1_weight: bfloat16 [2, 768, 3072], P('section', None, 'tensor'), may hold values from -0.21875 to 0.21875
- fc1_bias: float32 [2, 3072], P('section', 'tensor'), may hold values from -1.5 to 1.5
- fc2_weight: bfloat16 [2, 3072, 768], P('section', 'tensor'), may hold values from -0.109375 to 0.109375
- fc2_bias: float32 [2, 768], P('section'), may hold values from -1.5 to 1.5
- cotangent: bfloat16 [48, 577, 768], P('dp', None, 'tensor'), may hold values from -6 to 6
Outputs:
- activations: bfloat16 [2, 48, 577, 768], P('section', 'dp', None, 'tensor')
- input_grads: float32 [2, 48, 577, 768], P('section', 'dp', None, 'tensor')
- ln1_gain_grad: float32 [2, 768], P('section', 'tensor')
- ln1_bias_grad: float32 [2, 768], P('section', 'tensor')
- qkv_weight_grad: float32 [2, 768, 3, 768], P('section', None, None, 'tensor')
- qv_bias_grad: float32 [2, 2, 768], P('section', None, 'tensor')
- out_weight_grad: float32 [2, 768, 768], P('section', 'tensor')
- out_bias_grad: float32 [2, 768], P('section', 'tensor')
- ln2_gain_grad: float32 [2, 768], P('section', 'tensor')
- ln2_bias_grad: float32 [2, 768], P('section', 'tensor')
- fc1_weight_grad: float32 [2, 768, 3072], P('section', None, 'tensor')
- fc1_bias_grad: float32 [2, 3072], P('section', 'tensor')
- fc2_weight_grad: float32 [2, 3072, 768], P('section', 'tensor')
- fc2_bias_grad: float32 [2, 768], P('section', 'tensor')
Inputs may be any that keep to these rules, and one draw needn't show every extreme that they name: `slot_table`: within one data member's 2 entries, values below 3 are distinct; the value 3 means that the micro-batch has no image there.
All inputs are finite; a program needn't handle non-finite values.
Results may differ from a plain program's by a relative error of at most 0.0095.
Values may be sent and summed in bfloat16 or wider, within the bound.
No kernel may reach another device: no remote copies, remote signals or barrier semaphores. Data moves between devices by JAX's collectives and lax.ppermute only.
A program may use at most 192 MiB of HBM per device.

v0:
```python
from functools import partial
import jax
import jax.numpy as jnp
from jax import lax
from jax.sharding import PartitionSpec as P

HD = 64
epsilon = 1e-06


def shifted(block, axis, distance):
    devices = range(lax.axis_size(axis))
    route = [(i - distance, i) for i in devices if i - distance in devices]
    return lax.ppermute(block, axis, route)


def standardize_rows(values):
    row_means = jnp.mean(values, axis=1, keepdims=True)
    center = values - row_means
    inverse = lax.rsqrt(jnp.mean(center * center, axis=1, keepdims=True) + epsilon)
    return (center * inverse, row_means, inverse)


def contract_rows(left_side, right_side):
    return lax.dot_general(
        left_side, right_side, (((0,), (0,)), ((), ())), preferred_element_type=jnp.float32
    )


def contract_cols(left_side, right_side):
    return lax.dot_general(
        left_side, right_side, (((1,), (1,)), ((), ())), preferred_element_type=jnp.float32
    )


def member_sum(gradients):
    return lax.psum(gradients, "dp")


def tensor_scatter_sum(partial_value):
    group = lax.axis_size("tensor")
    rows_count, full_width = partial_value.shape
    pieces = lax.all_to_all(partial_value.astype(jnp.bfloat16), "tensor", 1, 0, tiled=True).reshape(
        group, rows_count, full_width // group
    )
    return jnp.sum(pieces.astype(jnp.float32), axis=0)


def tensor_sum(partial_value):
    summed = tensor_scatter_sum(partial_value)
    return lax.all_gather(summed.astype(jnp.bfloat16), "tensor", axis=1, tiled=True).astype(
        jnp.float32
    )


def layer_forward(partial_residual, params, column):
    (
        first_norm_gain,
        first_norm_bias,
        qkv_mat,
        qv_add,
        out_mat,
        out_add,
        second_norm_gain,
        second_norm_bias,
        up_mat,
        up_add,
        down_mat,
        down_add,
    ) = params
    rows_count = partial_residual.shape[0]
    part_width = partial_residual.shape[1]
    hidden_width = first_norm_gain.shape[0]
    head_count = part_width // HD
    complete_residual = lax.all_gather(partial_residual, "tensor", axis=1, tiled=True).astype(
        jnp.float32
    )
    first_centered_unit, first_row_averages, first_inverse_deviation = standardize_rows(
        complete_residual
    )
    first_normalized = (first_centered_unit * first_norm_gain + first_norm_bias).astype(
        jnp.bfloat16
    )
    projected = jnp.dot(
        first_normalized,
        qkv_mat.reshape(hidden_width, 3 * part_width),
        preferred_element_type=jnp.float32,
    ).reshape(rows_count, 3, part_width)
    queries = (projected[:, 0] + qv_add[0]).astype(jnp.bfloat16).reshape(rows_count, head_count, HD)
    keys_part = projected[:, 1].astype(jnp.bfloat16).reshape(rows_count, head_count, HD)
    values_part = (
        (projected[:, 2] + qv_add[1]).astype(jnp.bfloat16).reshape(rows_count, head_count, HD)
    )
    scores = jnp.einsum(
        "qhd,khd->hqk", queries, keys_part, preferred_element_type=jnp.float32
    ) * HD ** (-0.5)
    totals = jax.nn.logsumexp(scores, axis=2, keepdims=True)
    probabilities = jnp.exp(scores - totals)
    attended = (
        jnp.einsum(
            "hqk,khd->qhd",
            probabilities.astype(jnp.bfloat16),
            values_part,
            preferred_element_type=jnp.float32,
        )
        .reshape(rows_count, part_width)
        .astype(jnp.bfloat16)
    )
    branch = tensor_sum(jnp.dot(attended, out_mat, preferred_element_type=jnp.float32))
    middle = complete_residual + branch + out_add
    middle_rounded = middle.astype(jnp.bfloat16).astype(jnp.float32)
    second_centered_unit, second_row_averages, second_inverse_deviation = standardize_rows(
        middle_rounded
    )
    second_normalized = (second_centered_unit * second_norm_gain + second_norm_bias).astype(
        jnp.bfloat16
    )
    hidden_pre = jnp.dot(second_normalized, up_mat, preferred_element_type=jnp.float32) + up_add
    hidden = jax.nn.gelu(hidden_pre, approximate=False).astype(jnp.bfloat16)
    feed_out = tensor_scatter_sum(jnp.dot(hidden, down_mat, preferred_element_type=jnp.float32))
    result_part = (
        lax.dynamic_slice_in_dim(middle, column, part_width, 1)
        + feed_out
        + lax.dynamic_slice_in_dim(down_add, column, part_width, 0)
    )
    saved_state = (
        first_centered_unit,
        first_inverse_deviation,
        first_normalized,
        queries,
        keys_part,
        values_part,
        totals,
        attended,
        second_centered_unit,
        second_inverse_deviation,
        second_normalized,
        hidden_pre,
        hidden,
    )
    return (result_part.astype(jnp.bfloat16), saved_state)


def layer_backward(grad_part, saved_state, params, column, grad_sums):
    (
        first_norm_gain,
        first_norm_bias,
        qkv_mat,
        qv_add,
        out_mat,
        out_add,
        second_norm_gain,
        second_norm_bias,
        up_mat,
        up_add,
        down_mat,
        down_add,
    ) = params
    (
        first_centered_unit,
        first_inverse_deviation,
        first_normalized,
        queries,
        keys_part,
        values_part,
        totals,
        attended,
        second_centered_unit,
        second_inverse_deviation,
        second_normalized,
        hidden_pre,
        hidden,
    ) = saved_state
    rows_count = grad_part.shape[0]
    part_width = grad_part.shape[1]
    hidden_width = first_norm_gain.shape[0]
    head_count = part_width // HD

    def local_cols(matrix):
        return lax.dynamic_slice_in_dim(matrix, column, part_width, 1)

    grad_full_bf16 = lax.all_gather(grad_part, "tensor", axis=1, tiled=True)
    grad_full = grad_full_bf16.astype(jnp.float32)
    down_grad = contract_rows(hidden, grad_full_bf16)
    down_add_grad = jnp.sum(local_cols(grad_full), axis=0)
    hidden_grad = contract_cols(grad_full_bf16, down_mat)
    unused_value, gelu_back = jax.vjp(partial(jax.nn.gelu, approximate=False), hidden_pre)
    pre_grad = gelu_back(hidden_grad)[0].astype(jnp.bfloat16)
    up_grad = contract_rows(second_normalized, pre_grad)
    up_add_grad = jnp.sum(pre_grad.astype(jnp.float32), axis=0)
    normalized_gradient = tensor_sum(contract_cols(pre_grad, up_mat))
    second_gain_gradient = jnp.sum(local_cols(normalized_gradient * second_centered_unit), axis=0)
    bias_two_grad = jnp.sum(local_cols(normalized_gradient), axis=0)
    second_rescaled = normalized_gradient * second_norm_gain
    first_running_total = jnp.sum(second_rescaled, axis=1, keepdims=True)
    second_running_total = jnp.sum(second_rescaled * second_centered_unit, axis=1, keepdims=True)
    middle_grad = grad_full + second_inverse_deviation * (
        second_rescaled
        - first_running_total / hidden_width
        - second_centered_unit * second_running_total / hidden_width
    )
    feed_grads = (
        second_gain_gradient,
        bias_two_grad,
        up_grad,
        up_add_grad,
        down_grad,
        down_add_grad,
    )
    feed_grads = tuple((older + newer for older, newer in zip(grad_sums[6:], feed_grads)))
    branch_grad = middle_grad.astype(jnp.bfloat16)
    out_grad = contract_rows(attended, branch_grad)
    out_add_grad = jnp.sum(local_cols(middle_grad), axis=0)
    attended_grad = (
        contract_cols(branch_grad, out_mat).astype(jnp.bfloat16).reshape(rows_count, head_count, HD)
    )
    scale_factor = HD ** (-0.5)
    scores = (
        jnp.einsum("qhd,khd->hqk", queries, keys_part, preferred_element_type=jnp.float32)
        * scale_factor
    )
    probabilities = jnp.exp(scores - totals)
    values_grad = jnp.einsum(
        "hqk,qhd->khd",
        probabilities.astype(jnp.bfloat16),
        attended_grad,
        preferred_element_type=jnp.float32,
    )
    weight_grad = jnp.einsum(
        "qhd,khd->hqk", attended_grad, values_part, preferred_element_type=jnp.float32
    )
    rowdot = jnp.sum(probabilities * weight_grad, axis=2, keepdims=True)
    score_grad = (probabilities * (weight_grad - rowdot)).astype(jnp.bfloat16)
    query_grad = (
        jnp.einsum("hqk,khd->qhd", score_grad, keys_part, preferred_element_type=jnp.float32)
        * scale_factor
    )
    key_grad = (
        jnp.einsum("hqk,qhd->khd", score_grad, queries, preferred_element_type=jnp.float32)
        * scale_factor
    )
    projected_grad = jnp.stack(
        [
            query_grad.reshape(rows_count, part_width),
            key_grad.reshape(rows_count, part_width),
            values_grad.reshape(rows_count, part_width),
        ],
        axis=1,
    ).astype(jnp.bfloat16)
    flat_grad = projected_grad.reshape(rows_count, 3 * part_width)
    qkv_grad = contract_rows(first_normalized, flat_grad).reshape(hidden_width, 3, part_width)
    qv_add_grad = jnp.stack(
        [
            jnp.sum(projected_grad[:, 0].astype(jnp.float32), axis=0),
            jnp.sum(projected_grad[:, 2].astype(jnp.float32), axis=0),
        ]
    )
    first_normalized_gradient = tensor_sum(
        contract_cols(flat_grad, qkv_mat.reshape(hidden_width, 3 * part_width))
    )
    first_gain_gradient = jnp.sum(
        local_cols(first_normalized_gradient * first_centered_unit), axis=0
    )
    bias_one_grad = jnp.sum(local_cols(first_normalized_gradient), axis=0)
    first_rescaled = first_normalized_gradient * first_norm_gain
    third_running_total = jnp.sum(first_rescaled, axis=1, keepdims=True)
    fourth_running_total = jnp.sum(first_rescaled * first_centered_unit, axis=1, keepdims=True)
    stream_grad = middle_grad + first_inverse_deviation * (
        first_rescaled
        - third_running_total / hidden_width
        - first_centered_unit * fourth_running_total / hidden_width
    )
    attention_grads = (
        first_gain_gradient,
        bias_one_grad,
        qkv_grad,
        qv_add_grad,
        out_grad,
        out_add_grad,
    )
    attention_grads = tuple((older + newer for older, newer in zip(grad_sums[:6], attention_grads)))
    return (local_cols(stream_grad), attention_grads + feed_grads)


def shards(
    images,
    slot_table,
    ln1_gain,
    ln1_bias,
    qkv_weight,
    qv_bias,
    out_weight,
    out_bias,
    ln2_gain,
    ln2_bias,
    fc1_weight,
    fc1_bias,
    fc2_weight,
    fc2_bias,
    cotangent,
):
    params = tuple(
        (
            weight_arg[0]
            for weight_arg in (
                ln1_gain,
                ln1_bias,
                qkv_weight,
                qv_bias,
                out_weight,
                out_bias,
                ln2_gain,
                ln2_bias,
                fc1_weight,
                fc1_bias,
                fc2_weight,
                fc2_bias,
            )
        )
    )
    section_index = lax.axis_index("section")
    part_width = images.shape[2]
    column = lax.axis_index("tensor") * part_width
    slot_count = images.shape[0]
    micro_count = slot_table.shape[0]
    slot_ids = jnp.arange(slot_count, dtype=jnp.int32)

    def locate(batch_index):
        clipped = jnp.clip(batch_index, 0, micro_count - 1)
        chosen = lax.dynamic_index_in_dim(slot_table, clipped, 0, keepdims=False)
        active = (batch_index >= 0) & (batch_index < micro_count) & (chosen < slot_count)
        return (jnp.minimum(chosen, slot_count - 1), active, (slot_ids == chosen) & active)

    received = jnp.zeros(images.shape[1:], jnp.bfloat16)
    layer_outputs = jnp.zeros(images.shape, jnp.bfloat16)
    saved_states = []
    for step_index in range(micro_count + 1):
        where_from, active, placed = locate(step_index - section_index)
        own_image = lax.dynamic_index_in_dim(images, where_from, 0, keepdims=False)
        entering = jnp.where(section_index == 0, own_image, received)
        leaving, layer_state = layer_forward(entering, params, column)
        saved_states.append(layer_state)
        layer_outputs = layer_outputs + placed[:, None, None].astype(jnp.bfloat16) * leaving[None]
        if step_index < micro_count:
            received = shifted(leaving, "section", 1)

    def zeros_of(extent):
        return jnp.zeros(extent, jnp.float32)

    grad_sums = (
        zeros_of((part_width,)),
        zeros_of((part_width,)),
        zeros_of(params[2].shape),
        zeros_of(params[3].shape),
        zeros_of(params[4].shape),
        zeros_of((part_width,)),
        zeros_of((part_width,)),
        zeros_of((part_width,)),
        zeros_of(params[8].shape),
        zeros_of(params[9].shape),
        zeros_of(params[10].shape),
        zeros_of((part_width,)),
    )
    coming_back = jnp.zeros(images.shape[1:], jnp.bfloat16)
    grads_in = jnp.zeros(images.shape, jnp.float32)
    for step_index in range(micro_count + 1):
        where_from, active, placed = locate(micro_count - step_index - section_index)
        own_grad = lax.dynamic_index_in_dim(cotangent, where_from, 0, keepdims=False)
        entering = jnp.where(
            active, jnp.where(section_index == 1, own_grad, coming_back), jnp.zeros_like(own_grad)
        )
        stream_grad, grad_sums = layer_backward(
            entering, saved_states[micro_count - step_index], params, column, grad_sums
        )
        grads_in = grads_in + placed[:, None, None].astype(jnp.float32) * stream_grad[None]
        if step_index < micro_count:
            coming_back = shifted(stream_grad.astype(jnp.bfloat16), "section", -1)
    flat_sums = member_sum(jnp.concatenate([gradient.reshape(-1) for gradient in grad_sums]))
    unpacked = []
    offset = 0
    for gradient in grad_sums:
        unpacked.append(flat_sums[offset : offset + gradient.size].reshape(gradient.shape))
        offset += gradient.size
    grad_sums = tuple(unpacked)
    return (layer_outputs[None], grads_in[None]) + tuple((gradient[None] for gradient in grad_sums))


def solution(mesh):
    in_specs = (
        P("dp", None, "tensor"),
        P("dp"),
        P("section", None),
        P("section", None),
        P("section", None, None, "tensor"),
        P("section", None, "tensor"),
        P("section", "tensor", None),
        P("section", None),
        P("section", None),
        P("section", None),
        P("section", None, "tensor"),
        P("section", "tensor"),
        P("section", "tensor", None),
        P("section", None),
        P("dp", None, "tensor"),
    )
    out_specs = (
        P("section", "dp", None, "tensor"),
        P("section", "dp", None, "tensor"),
        P("section", "tensor"),
        P("section", "tensor"),
        P("section", None, None, "tensor"),
        P("section", None, "tensor"),
        P("section", "tensor", None),
        P("section", "tensor"),
        P("section", "tensor"),
        P("section", "tensor"),
        P("section", None, "tensor"),
        P("section", "tensor"),
        P("section", "tensor", None),
        P("section", "tensor"),
    )
    return jax.shard_map(shards, mesh=mesh, in_specs=in_specs, out_specs=out_specs, check_vma=False)
```

profile of v0, /device:TPU:1, one launch (start us, length us, event | category | flops | bytes accessed | tf_op | source)
XLA Modules:
  0.0 821.9 jit_solution(293552219122720393)
XLA Ops:
  11.7 13.4 %all-gather = bf16[1,577,768]{1,2,0:T(8,128)(2,1)S(1)} all-gather(bf16[1,577,192]{1,2,0:T(8,128)(2,1)S(1)} %dynamic-slice_select_fusion), channel_id=2, replica_groups=mesh['section'=2,'dp'=16,'tensor'=4] {'tensor'}, dimensions={2}, use_global_device_ids=true | all-gather | bytes 1107840 | tf_op jit(solution)/shard_map/all_gather | solution.py:75
  39.7 14.4 %all-to-all-done = bf16[577,4,192]{0,2,1:T(8,128)(2,1)} async-done(((bf16[577,4,192]{0,2,1:T(8,128)(2,1)}), bf16[577,4,192]{0,2,1:T(8,128)(2,1)}, u32[]{:S(2)}, u32[]{:S(2)}) %all-to-all-start) | async-done | bytes 886304 | tf_op jit(solution)/shard_map/all_to_all | solution.py:43
  55.5 11.6 %all_gather.46 = bf16[577,768]{0,1:T(8,128)(2,1)S(1)} all-gather(bf16[577,192]{0,1:T(8,128)(2,1)S(1)} %reduce_sum.651), channel_id=1, replica_groups=mesh['section'=2,'dp'=16,'tensor'=4] {'tensor'}, dimensions={1}, use_global_device_ids=true | all-gather | bytes 1107840 | tf_op jit(solution)/shard_map/all_gather | solution.py:51
  83.2 13.6 %all-to-all-done.1 = bf16[577,4,192]{0,2,1:T(8,128)(2,1)S(1)} async-done(((bf16[577,4,192]{0,2,1:T(8,128)(2,1)}), bf16[577,4,192]{0,2,1:T(8,128)(2,1)S(1)}, u32[]{:S(2)}, u32[]{:S(2)}) %all-to-all-start.1) | async-done | bytes 886304 | tf_op jit(solution)/shard_map/all_to_all | solution.py:43
  106.2 11.6 %all_gather.47 = bf16[577,768]{0,1:T(8,128)(2,1)S(1)} all-gather(bf16[577,192]{0,1:T(8,128)(2,1)S(1)} %bitcast_select_fusion.3), channel_id=1, replica_groups=mesh['section'=2,'dp'=16,'tensor'=4] {'tensor'}, dimensions={1}, use_global_device_ids=true | all-gather | bytes 1107840 | tf_op jit(solution)/shard_map/all_gather | solution.py:75
  127.2 17.9 %all_to_all.156 = bf16[577,4,192]{0,2,1:T(8,128)(2,1)} all-to-all(bf16[577,4,192]{0,2,1:T(8,128)(2,1)S(1)} %bitcast.295), channel_id=1, replica_groups=mesh['section'=2,'dp'=16,'tensor'=4] {'tensor'}, dimensions={1} | all-to-all | bytes 1772544 | tf_op jit(solution)/shard_map/all_to_all | solution.py:43
  146.5 11.9 %all_gather.48 = bf16[577,768]{0,1:T(8,128)(2,1)S(1)} all-gather(bf16[577,192]{0,1:T(8,128)(2,1)S(1)} %reduce_sum.658), channel_id=1, replica_groups=mesh['section'=2,'dp'=16,'tensor'=4] {'tensor'}, dimensions={1}, use_global_device_ids=true | all-gather | bytes 1107840 | tf_op jit(solution)/shard_map/all_gather | solution.py:51
  171.2 17.1 %all_to_all.157 = bf16[577,4,192]{0,2,1:T(8,128)(2,1)S(1)} all-to-all(bf16[577,4,192]{0,2,1:T(8,128)(2,1)S(1)} %bitcast.296), channel_id=1, replica_groups=mesh['section'=2,'dp'=16,'tensor'=4] {'tensor'}, dimensions={1} | all-to-all | bytes 1772544 | tf_op jit(solution)/shard_map/all_to_all | solution.py:43
  199.2 11.5 %all_gather.49 = bf16[577,768]{0,1:T(8,128)(2,1)S(1)} all-gather(bf16[577,192]{0,1:T(8,128)(2,1)S(1)} %bitcast_select_fusion.2), channel_id=1, replica_groups=mesh['section'=2,'dp'=16,'tensor'=4] {'tensor'}, dimensions={1}, use_global_device_ids=true | all-gather | bytes 1107840 | tf_op jit(solution)/shard_map/all_gather | solution.py:75
  226.8 20.1 %all-gather.1 = bf16[1,577,768]{1,2,0:T(8,128)(2,1)} all-gather(bf16[1,577,192]{1,2,0:T(8,128)(2,1)S(1)} %select_select_fusion), channel_id=3, replica_groups=mesh['section'=2,'dp'=16,'tensor'=4] {'tensor'}, dimensions={2}, use_global_device_ids=true | all-gather | bytes 1107840 | tf_op jit(solution)/shard_map/all_gather | solution.py:182
  248.3 11.5 %all_gather.50 = bf16[577,768]{0,1:T(8,128)(2,1)S(1)} all-gather(bf16[577,192]{0,1:T(8,128)(2,1)S(1)} %reduce_sum.665), channel_id=1, replica_groups=mesh['section'=2,'dp'=16,'tensor'=4] {'tensor'}, dimensions={1}, use_global_device_ids=true | all-gather | bytes 1107840 | tf_op jit(solution)/shard_map/all_gather | solution.py:51
  281.6 11.9 %all-to-all-done.6 = bf16[577,4,192]{0,2,1:T(8,128)(2,1)} async-done(((bf16[577,4,192]{0,2,1:T(8,128)(2,1)}), bf16[577,4,192]{0,2,1:T(8,128)(2,1)}, u32[]{:S(2)}, u32[]{:S(2)}) %all-to-all-start.6) | async-done | bytes 886304 | tf_op jit(solution)/shard_map/all_to_all | solution.py:43
  295.6 12.1 %all_gather.52 = bf16[577,768]{0,1:T(8,128)(2,1)S(1)} all-gather(bf16[577,192]{0,1:T(8,128)(2,1)} %reduce_sum.669), channel_id=1, replica_groups=mesh['section'=2,'dp'=16,'tensor'=4] {'tensor'}, dimensions={1}, use_global_device_ids=true | all-gather | bytes 1107840 | tf_op jit(solution)/shard_map/all_gather | solution.py:51
  344.0 11.3 %all_gather.53 = bf16[577,768]{0,1:T(8,128)(2,1)S(1)} all-gather(bf16[577,192]{0,1:T(8,128)(2,1)S(1)} %reduce_sum.673), channel_id=1, replica_groups=mesh['section'=2,'dp'=16,'tensor'=4] {'tensor'}, dimensions={1}, use_global_device_ids=true | all-gather | bytes 1107840 | tf_op jit(solution)/shard_map/all_gather | solution.py:51
  369.3 11.5 %all_gather.54 = bf16[577,768]{0,1:T(8,128)(2,1)S(1)} all-gather(bf16[577,192]{0,1:T(8,128)(2,1)S(1)} %fusion.126), channel_id=1, replica_groups=mesh['section'=2,'dp'=16,'tensor'=4] {'tensor'}, dimensions={1}, use_global_device_ids=true | all-gather | bytes 1107840 | tf_op jit(solution)/shard_map/all_gather | solution.py:182
  408.9 11.6 %all_gather.55 = bf16[577,768]{0,1:T(8,128)(2,1)S(1)} all-gather(bf16[577,192]{0,1:T(8,128)(2,1)} %reduce_sum.676), channel_id=1, replica_groups=mesh['section'=2,'dp'=16,'tensor'=4] {'tensor'}, dimensions={1}, use_global_device_ids=true | all-gather | bytes 1107840 | tf_op jit(solution)/shard_map/all_gather | solution.py:51
  446.9 7.1 all-to-all-done.9
  455.4 11.3 %all_gather.56 = bf16[577,768]{0,1:T(8,128)(2,1)S(1)} all-gather(bf16[577,192]{0,1:T(8,128)(2,1)S(1)} %reduce_sum.680), channel_id=1, replica_groups=mesh['section'=2,'dp'=16,'tensor'=4] {'tensor'}, dimensions={1}, use_global_device_ids=true | all-gather | bytes 1107840 | tf_op jit(solution)/shard_map/all_gather | solution.py:51
  480.4 11.7 %all_gather.57 = bf16[577,768]{0,1:T(8,128)(2,1)S(1)} all-gather(bf16[577,192]{0,1:T(8,128)(2,1)S(1)} %fusion.125), channel_id=1, replica_groups=mesh['section'=2,'dp'=16,'tensor'=4] {'tensor'}, dimensions={1}, use_global_device_ids=true | all-gather | bytes 1107840 | tf_op jit(solution)/shard_map/all_gather | solution.py:182
  523.1 11.7 %all_gather.58 = bf16[577,768]{0,1:T(8,128)(2,1)S(1)} all-gather(bf16[577,192]{0,1:T(8,128)(2,1)} %reduce_sum.683), channel_id=1, replica_groups=mesh['section'=2,'dp'=16,'tensor'=4] {'tensor'}, dimensions={1}, use_global_device_ids=true | all-gather | bytes 1107840 | tf_op jit(solution)/shard_map/all_gather | solution.py:51
  574.7 11.7 %all_gather.59 = bf16[577,768]{0,1:T(8,128)(2,1)S(1)} all-gather(bf16[577,192]{0,1:T(8,128)(2,1)S(1)} %reduce_sum.687), channel_id=1, replica_groups=mesh['section'=2,'dp'=16,'tensor'=4] {'tensor'}, dimensions={1}, use_global_device_ids=true | all-gather | bytes 1107840 | tf_op jit(solution)/shard_map/all_gather | solution.py:51
  592.1 64.9 %concatenate.3 = f32[1771776]{0:T(1024)} concatenate(f32[192]{0:T(256)} %add_add_fusion.9, f32[192]{0:T(256)} %add_add_fusion.8, f32[442368]{0:T(1024)} %reshape.471, f32[384]{0:T(512)S(1)} %add.509, f32[147456]{0:T(1024)} %reshape.472, f32[192]{0:T(256)S(1)} %add_add_fusion.7, f32[192]{0:T(256)} %add_add_fusion.6, f32[192]{0:T(256)} %add_add_fusion.5, f32[589824]{0:T(1024)S(1)} %copy-done.30, ...), dimensions={0} | concatenate | bytes 14174208 | tf_op jit(solution)/shard_map/concatenate | solution.py:378
  668.2 12.4 %all-to-all-done.5 = bf16[577,4,192]{0,2,1:T(8,128)(2,1)S(1)} async-done(((bf16[577,4,192]{0,2,1:T(8,128)(2,1)}), bf16[577,4,192]{0,2,1:T(8,128)(2,1)S(1)}, u32[]{:S(2)}, u32[]{:S(2)}) %all-to-all-start.5) | async-done | bytes 886304 | tf_op jit(solution)/shard_map/all_to_all | solution.py:43
  684.4 102.6 %all-reduce.2.cloned.1.call-done = f32[1771776]{0:T(1024)} async-done(((f32[1771776]{0:T(1024)}), f32[1771776]{0:T(1024)}) %all-reduce.2.cloned.1.call-update) | async-done | bytes 7087120 | tf_op jit(solution)/shard_map/psum | solution.py:37
  (534 shorter events, 355.7 us)
Async XLA Ops:
  7.2 62.0 %copy-start = (bf16[1,768,768]{2,1,0:T(8,128)(2,1)S(1)}, bf16[1,768,768]{2,1,0:T(8,128)(2,1)}, u32[]{:S(2)}) copy-start(bf16[1,768,768]{2,1,0:T(8,128)(2,1)} %param.25) | copy-start | bytes 3538948
  25.1 42.0 %copy-start.4 = (bf16[1,577,768]{1,2,0:T(8,128)(2,1)}, bf16[1,577,768]{1,2,0:T(8,128)(2,1)S(1)}, u32[]{:S(2)}) copy-start(bf16[1,577,768]{1,2,0:T(8,128)(2,1)S(1)} %all-gather) | copy-start | bytes 2658820
  35.3 18.9 %all-to-all-start = ((bf16[577,4,192]{0,2,1:T(8,128)(2,1)}), bf16[577,4,192]{0,2,1:T(8,128)(2,1)}, u32[]{:S(2)}, u32[]{:S(2)}) async-start(bf16[577,4,192]{0,2,1:T(8,128)(2,1)} %bitcast.293), calls=%async_computation | async-start | bytes 1966080 | tf_op jit(solution)/shard_map/all_to_all | solution.py:43
  78.8 18.0 %all-to-all-start.1 = ((bf16[577,4,192]{0,2,1:T(8,128)(2,1)}), bf16[577,4,192]{0,2,1:T(8,128)(2,1)S(1)}, u32[]{:S(2)}, u32[]{:S(2)}) async-start(bf16[577,4,192]{0,2,1:T(8,128)(2,1)} %bitcast.15), calls=%async_computation.1 | async-start | bytes 1966080 | tf_op jit(solution)/shard_map/all_to_all | solution.py:43
  98.2 7.0 collective-permute-start
  189.6 21.6 %copy-start.80 = (bf16[577,192]{0,1:T(8,128)(2,1)}, bf16[577,192]{0,1:T(8,128)(2,1)S(1)}, u32[]{:S(2)}) copy-start(bf16[577,192]{0,1:T(8,128)(2,1)S(1)} %add_convert_fusion.12) | copy-start | bytes 664708
  189.6 8.6 %collective-permute-start.1 = (bf16[577,192]{0,1:T(8,128)(2,1)S(1)}, bf16[577,192]{0,1:T(8,128)(2,1)S(1)}, u32[]{:S(2)}, u32[]{:S(2)}) collective-permute-start(bf16[577,192]{0,1:T(8,128)(2,1)S(1)} %add_convert_fusion.12), channel_id=1, source_target_pairs={{0,64},{1,65},{2,66},{3,67},{4,68},{5,69},{6,70},{7,71},{8,72},{9,... | collective-permute-start | bytes 664712 | tf_op jit(solution)/shard_map/ppermute | solution.py:14
  220.8 26.1 %all-to-all-start.4 = ((bf16[577,4,192]{0,2,1:T(8,128)(2,1)}), bf16[577,4,192]{0,2,1:T(8,128)(2,1)}, u32[]{:S(2)}, u32[]{:S(2)}) async-start(bf16[577,4,192]{0,2,1:T(8,128)(2,1)} %bitcast.292), calls=%async_computation.4 | async-start | bytes 1966080 | tf_op jit(solution)/shard_map/all_to_all | solution.py:43
  274.7 18.8 %all-to-all-start.6 = ((bf16[577,4,192]{0,2,1:T(8,128)(2,1)}), bf16[577,4,192]{0,2,1:T(8,128)(2,1)}, u32[]{:S(2)}, u32[]{:S(2)}) async-start(bf16[577,4,192]{0,2,1:T(8,128)(2,1)} %bitcast.294), calls=%async_computation.6 | async-start | bytes 1966080 | tf_op jit(solution)/shard_map/all_to_all | solution.py:43
  279.0 34.7 %slice-start.4 = ((s8[4485120]{0:T(1024)(128)(4,1)}), s8[290816]{0:T(1024)(128)(4,1)S(1)}, s32[]{:S(2)}) async-start(s8[4485120]{0:T(1024)(128)(4,1)} %bitcast.273), calls=%async_computation.17 | async-start | bytes 581632
  323.7 18.8 %all-to-all-start.7 = ((bf16[577,4,192]{0,2,1:T(8,128)(2,1)}), bf16[577,4,192]{0,2,1:T(8,128)(2,1)}, u32[]{:S(2)}, u32[]{:S(2)}) async-start(bf16[577,4,192]{0,2,1:T(8,128)(2,1)} %bitcast.288), calls=%async_computation.7 | async-start | bytes 1966080 | tf_op jit(solution)/shard_map/all_to_all | solution.py:43
  358.7 9.5 %collective-permute-start.2 = (bf16[577,192]{0,1:T(8,128)(2,1)S(1)}, bf16[577,192]{0,1:T(8,128)(2,1)S(1)}, u32[]{:S(2)}, u32[]{:S(2)}) collective-permute-start(bf16[577,192]{0,1:T(8,128)(2,1)S(1)} %get-tuple-element.62), channel_id=1, source_target_pairs={{64,0},{65,1},{66,2},{67,3},{68,4},{69,5},{70,6},{71,7},{72,8},{73... | collective-permute-start | bytes 664712 | tf_op jit(solution)/shard_map/ppermute | solution.py:14
  360.0 20.7 %copy-start.140 = (f32[577,768]{1,0:T(8,128)S(1)}, f32[577,768]{1,0:T(8,128)}, u32[]{:S(2)}) copy-start(f32[577,768]{1,0:T(8,128)} %get-tuple-element.70) | copy-start | bytes 5317636
  360.1 20.7 %copy-start.141 = (f32[577,768]{1,0:T(8,128)S(1)}, f32[577,768]{1,0:T(8,128)}, u32[]{:S(2)}) copy-start(f32[577,768]{1,0:T(8,128)} %get-tuple-element.120) | copy-start | bytes 5317636
  387.9 18.9 %all-to-all-start.8 = ((bf16[577,4,192]{0,2,1:T(8,128)(2,1)}), bf16[577,4,192]{0,2,1:T(8,128)(2,1)}, u32[]{:S(2)}, u32[]{:S(2)}) async-start(bf16[577,4,192]{0,2,1:T(8,128)(2,1)} %bitcast.290), calls=%async_computation.8 | async-start | bytes 1966080 | tf_op jit(solution)/shard_map/all_to_all | solution.py:43
  398.9 26.1 %slice-start.2 = ((s8[4485120]{0:T(1024)(128)(4,1)}), s8[290816]{0:T(1024)(128)(4,1)S(1)}, s32[]{:S(2)}) async-start(s8[4485120]{0:T(1024)(128)(4,1)} %bitcast.271), calls=%async_computation.15 | async-start | bytes 581632
  435.1 18.9 %all-to-all-start.9 = ((bf16[577,4,192]{0,2,1:T(8,128)(2,1)}), bf16[577,4,192]{0,2,1:T(8,128)(2,1)}, u32[]{:S(2)}, u32[]{:S(2)}) async-start(bf16[577,4,192]{0,2,1:T(8,128)(2,1)} %bitcast.291), calls=%async_computation.9 | async-start | bytes 1966080 | tf_op jit(solution)/shard_map/all_to_all | solution.py:43
  470.1 9.3 %collective-permute-start.3 = (bf16[577,192]{0,1:T(8,128)(2,1)S(1)}, bf16[577,192]{0,1:T(8,128)(2,1)S(1)}, u32[]{:S(2)}, u32[]{:S(2)}) collective-permute-start(bf16[577,192]{0,1:T(8,128)(2,1)S(1)} %get-tuple-element.60), channel_id=1, source_target_pairs={{64,0},{65,1},{66,2},{67,3},{68,4},{69,5},{70,6},{71,7},{72,8},{73... | collective-permute-start | bytes 664712 | tf_op jit(solution)/shard_map/ppermute | solution.py:14
  471.4 20.7 %copy-start.138 = (f32[577,768]{1,0:T(8,128)S(1)}, f32[577,768]{1,0:T(8,128)}, u32[]{:S(2)}) copy-start(f32[577,768]{1,0:T(8,128)} %get-tuple-element.75) | copy-start | bytes 5317636
  498.8 22.2 %all-to-all-start.10 = ((bf16[577,4,192]{0,2,1:T(8,128)(2,1)}), bf16[577,4,192]{0,2,1:T(8,128)(2,1)}, u32[]{:S(2)}, u32[]{:S(2)}) async-start(bf16[577,4,192]{0,2,1:T(8,128)(2,1)} %bitcast.289), calls=%async_computation.10 | async-start | bytes 1966080 | tf_op jit(solution)/shard_map/all_to_all | solution.py:43
  515.9 23.3 %slice-start = ((s8[4485120]{0:T(1024)(128)(4,1)}), s8[290816]{0:T(1024)(128)(4,1)S(1)}, s32[]{:S(2)}) async-start(s8[4485120]{0:T(1024)(128)(4,1)} %bitcast.269), calls=%async_computation.13 | async-start | bytes 581632
  549.6 23.7 %all-to-all-start.11 = ((bf16[577,4,192]{0,2,1:T(8,128)(2,1)}), bf16[577,4,192]{0,2,1:T(8,128)(2,1)}, u32[]{:S(2)}, u32[]{:S(2)}) async-start(bf16[577,4,192]{0,2,1:T(8,128)(2,1)} %bitcast.287), calls=%async_computation.11 | async-start | bytes 1966080 | tf_op jit(solution)/shard_map/all_to_all | solution.py:43
  554.0 233.1 %all-reduce.2.cloned.1.call-start = ((), (), s32[]{:S(2)}) async-start(), calls=%async_computation.12 | async-start | bytes 14180352 | tf_op jit(solution)/shard_map/psum | solution.py:37
  661.6 18.9 %all-to-all-start.5 = ((bf16[577,4,192]{0,2,1:T(8,128)(2,1)}), bf16[577,4,192]{0,2,1:T(8,128)(2,1)S(1)}, u32[]{:S(2)}, u32[]{:S(2)}) async-start(bf16[577,4,192]{0,2,1:T(8,128)(2,1)} %bitcast.38), calls=%async_computation.5 | async-start | bytes 1966080 | tf_op jit(solution)/shard_map/all_to_all | solution.py:43
  (139 other events, 591.1 us)
Sparse Core Ops, SparseCore 0:
  657.1 129.8 all-reduce.1
where the time goes:
time: 833 us; the launch traced here: 822 us
  blocking collectives  219 us (26%)
  waiting for transfers between devices  192 us (23%)
  local copies, waits for them, and re-layouts  157 us (19%)
  matrix products  99.9 us (12%)
  other arithmetic  82 us (10%)
  starting transfers between devices  52.3 us (6%)
  between operations  20 us (2%)
    all_gather x9, blocking collectives, tensor_sum(): lax.all_gather(summed.astype(jnp.bfloat16), 'tensor', axis=1, tiled=True)  105 us
    psum x1, waiting for transfers between devices, member_sum(): return lax.psum(gradients, 'dp')  103 us
    all_to_all x10, waiting for transfers between devices, tensor_scatter_sum(): lax.all_to_all(partial_value.astype(jnp.bfloat16), 'tensor', 1, 0, tiled=...  69.8 us
    concatenate x1, local copies, waits for them, and re-layouts, shards(): jnp.concatenate([gradient.reshape(-1) for gradient in grad_sums])  64.9 us
    all_gather x3, blocking collectives, layer_backward(): grad_full_bf16 = lax.all_gather(grad_part, 'tensor', axis=1, tiled=True)  43.2 us
    all_to_all x10, starting transfers between devices, tensor_scatter_sum(): lax.all_to_all(partial_value.astype(jnp.bfloat16), 'tensor', 1, 0, tiled=...  42.9 us
    all_gather x3, blocking collectives, layer_forward(): lax.all_gather(partial_residual, 'tensor', axis=1, tiled=True)  36.5 us
    dot_general x12, matrix products, contract_rows(): lax.dot_general(left_side, right_side, (((0,), (0,)), ((), ())), preferre...  35.1 us
  transfers between devices with their start and end apart: 15, of which 12 were waited for; matrix products, arithmetic and copies ran while one was open for 10% of the time, Pallas kernels for 0%

commit v1 on v0

--- a/solution.py
+++ b/solution.py
@@ -179,7 +179,9 @@
     def local_cols(matrix):
         return lax.dynamic_slice_in_dim(matrix, column, part_width, 1)
 
-    grad_full_bf16 = lax.all_gather(grad_part, "tensor", axis=1, tiled=True)
+    grad_full_bf16 = jnp.concatenate(
+        lax.all_to_all(jnp.stack([grad_part] * lax.axis_size("tensor")), "tensor", 0, 0), axis=1
+    )
     grad_full = grad_full_bf16.astype(jnp.float32)
     down_grad = contract_rows(hidden, grad_full_bf16)
     down_add_grad = jnp.sum(local_cols(grad_full), axis=0)

time: 833 us -> 863 us (1.036)
  waiting for transfers between devices: 192 us -> 206 us
    all_gather x3 -> x0, blocking collectives: 43.2 us -> none  [layer_backward(): grad_full_bf16 = lax.all_gather(grad_part, 'tensor', axis=1, tiled=True)]
    all_to_all x2 -> x4, blocking collectives: 35 us -> 73 us  [tensor_scatter_sum(): lax.all_to_all(partial_value.astype(jnp.bfloat16), 'tensor', 1, 0, tiled=...]
    all_to_all x0 -> x3, waiting for transfers between devices: none -> 20.5 us  [layer_backward(): lax.all_to_all(jnp.stack([grad_part] * lax.axis_size('tensor')), 'tensor'...]
    all_to_all x0 -> x3, starting transfers between devices: none -> 15.2 us  [layer_backward(): lax.all_to_all(jnp.stack([grad_part] * lax.axis_size('tensor')), 'tensor'...]
    all_to_all x10 -> x8, starting transfers between devices: 42.9 us -> 35.2 us  [tensor_scatter_sum(): lax.all_to_all(partial_value.astype(jnp.bfloat16), 'tensor', 1, 0, tiled=...]
    all_to_all x10 -> x8, waiting for transfers between devices: 69.8 us -> 63.6 us  [tensor_scatter_sum(): lax.all_to_all(partial_value.astype(jnp.bfloat16), 'tensor', 1, 0, tiled=...]
    unnamed x297 -> x249, local copies, waits for them, and re-layouts: 25.3 us -> 24.3 us
  transfers between devices with their start and end apart: 15 -> 16, of which waited for: 12 -> 13; matrix products, arithmetic and copies ran while one was open for 10% -> 11% of each run, Pallas kernels for 0% -> 0%
where the time goes in v1:
time: 863 us; the launch traced here: 852 us
  blocking collectives  222 us (26%)
  waiting for transfers between devices  206 us (24%)
  local copies, waits for them, and re-layouts  154 us (18%)
  matrix products  108 us (13%)
  other arithmetic  82.2 us (10%)
  starting transfers between devices  59.8 us (7%)
  between operations  19.9 us (2%)
    all_gather x9, blocking collectives, tensor_sum(): lax.all_gather(summed.astype(jnp.bfloat16), 'tensor', axis=1, tiled=True)  113 us
    psum x1, waiting for transfers between devices, member_sum(): return lax.psum(gradients, 'dp')  103 us
    all_to_all x4, blocking collectives, tensor_scatter_sum(): lax.all_to_all(partial_value.astype(jnp.bfloat16), 'tensor', 1, 0, tiled=...  73 us
    all_to_all x8, waiting for transfers between devices, tensor_scatter_sum(): lax.all_to_all(partial_value.astype(jnp.bfloat16), 'tensor', 1, 0, tiled=...  63.6 us
    concatenate x1, local copies, waits for them, and re-layouts, shards(): jnp.concatenate([gradient.reshape(-1) for gradient in grad_sums])  62.2 us
    all_gather x3, blocking collectives, layer_forward(): lax.all_gather(partial_residual, 'tensor', axis=1, tiled=True)  36.5 us
    dot_general x12, matrix products, contract_rows(): lax.dot_general(left_side, right_side, (((0,), (0,)), ((), ())), preferre...  36.3 us
    all_to_all x8, starting transfers between devices, tensor_scatter_sum(): lax.all_to_all(partial_value.astype(jnp.bfloat16), 'tensor', 1, 0, tiled=...  35.2 us
  transfers between devices with their start and end apart: 16, of which 13 were waited for; matrix products, arithmetic and copies ran while one was open for 11% of the time, Pallas kernels for 0%

profile of v1, /device:TPU:1, one launch (start us, length us, event | category | flops | bytes accessed | tf_op | source)
XLA Modules:
  0.0 852.0 jit_solution(11705163494429059157)
XLA Ops:
  11.7 13.4 %all-gather = bf16[1,577,768]{1,2,0:T(8,128)(2,1)S(1)} all-gather(bf16[1,577,192]{1,2,0:T(8,128)(2,1)S(1)} %dynamic-slice_select_fusion), channel_id=2, replica_groups=mesh['section'=2,'dp'=16,'tensor'=4] {'tensor'}, dimensions={2}, use_global_device_ids=true | all-gather | bytes 1107840 | tf_op jit(solution)/shard_map/all_gather | solution.py:75
  38.2 14.3 %all-to-all-done = bf16[577,4,192]{0,2,1:T(8,128)(2,1)S(1)} async-done(((bf16[577,4,192]{0,2,1:T(8,128)(2,1)}), bf16[577,4,192]{0,2,1:T(8,128)(2,1)S(1)}, u32[]{:S(2)}, u32[]{:S(2)}) %all-to-all-start) | async-done | bytes 886304 | tf_op jit(solution)/shard_map/all_to_all | solution.py:43
  53.4 11.7 %all_gather.37 = bf16[577,768]{0,1:T(8,128)(2,1)S(1)} all-gather(bf16[577,192]{0,1:T(8,128)(2,1)} %reduce_sum.651), channel_id=1, replica_groups=mesh['section'=2,'dp'=16,'tensor'=4] {'tensor'}, dimensions={1}, use_global_device_ids=true | all-gather | bytes 1107840 | tf_op jit(solution)/shard_map/all_gather | solution.py:51
  80.2 13.6 %all-to-all-done.1 = bf16[577,4,192]{0,2,1:T(8,128)(2,1)S(1)} async-done(((bf16[577,4,192]{0,2,1:T(8,128)(2,1)}), bf16[577,4,192]{0,2,1:T(8,128)(2,1)S(1)}, u32[]{:S(2)}, u32[]{:S(2)}) %all-to-all-start.1) | async-done | bytes 886304 | tf_op jit(solution)/shard_map/all_to_all | solution.py:43
  103.2 11.5 %all_gather.38 = bf16[577,768]{0,1:T(8,128)(2,1)S(1)} all-gather(bf16[577,192]{0,1:T(8,128)(2,1)S(1)} %bitcast_select_fusion.3), channel_id=1, replica_groups=mesh['section'=2,'dp'=16,'tensor'=4] {'tensor'}, dimensions={1}, use_global_device_ids=true | all-gather | bytes 1107840 | tf_op jit(solution)/shard_map/all_gather | solution.py:75
  124.0 17.9 %all_to_all.171 = bf16[577,4,192]{0,2,1:T(8,128)(2,1)} all-to-all(bf16[577,4,192]{0,2,1:T(8,128)(2,1)S(1)} %bitcast.297), channel_id=1, replica_groups=mesh['section'=2,'dp'=16,'tensor'=4] {'tensor'}, dimensions={1} | all-to-all | bytes 1772544 | tf_op jit(solution)/shard_map/all_to_all | solution.py:43
  143.3 11.5 %all_gather.39 = bf16[577,768]{0,1:T(8,128)(2,1)S(1)} all-gather(bf16[577,192]{0,1:T(8,128)(2,1)S(1)} %reduce_sum.658), channel_id=1, replica_groups=mesh['section'=2,'dp'=16,'tensor'=4] {'tensor'}, dimensions={1}, use_global_device_ids=true | all-gather | bytes 1107840 | tf_op jit(solution)/shard_map/all_gather | solution.py:51
  167.8 17.1 %all_to_all.172 = bf16[577,4,192]{0,2,1:T(8,128)(2,1)S(1)} all-to-all(bf16[577,4,192]{0,2,1:T(8,128)(2,1)S(1)} %bitcast.298), channel_id=1, replica_groups=mesh['section'=2,'dp'=16,'tensor'=4] {'tensor'}, dimensions={1} | all-to-all | bytes 1772544 | tf_op jit(solution)/shard_map/all_to_all | solution.py:43
  195.8 11.6 %all_gather.40 = bf16[577,768]{0,1:T(8,128)(2,1)S(1)} all-gather(bf16[577,192]{0,1:T(8,128)(2,1)S(1)} %bitcast_select_fusion.2), channel_id=1, replica_groups=mesh['section'=2,'dp'=16,'tensor'=4] {'tensor'}, dimensions={1}, use_global_device_ids=true | all-gather | bytes 1107840 | tf_op jit(solution)/shard_map/all_gather | solution.py:75
  223.4 12.9 %all-to-all-done.4 = bf16[577,4,192]{0,2,1:T(8,128)(2,1)} async-done(((bf16[577,4,192]{0,2,1:T(8,128)(2,1)}), bf16[577,4,192]{0,2,1:T(8,128)(2,1)}, u32[]{:S(2)}, u32[]{:S(2)}) %all-to-all-start.4) | async-done | bytes 886304 | tf_op jit(solution)/shard_map/all_to_all | solution.py:43
  243.8 19.9 %all_gather.41 = bf16[577,768]{0,1:T(8,128)(2,1)S(1)} all-gather(bf16[577,192]{0,1:T(8,128)(2,1)S(1)} %reduce_sum.665), channel_id=1, replica_groups=mesh['section'=2,'dp'=16,'tensor'=4] {'tensor'}, dimensions={1}, use_global_device_ids=true | all-gather | bytes 1107840 | tf_op jit(solution)/shard_map/all_gather | solution.py:51
  282.8 19.1 %all_to_all.173 = bf16[577,4,192]{0,2,1:T(8,128)(2,1)} all-to-all(bf16[577,4,192]{0,2,1:T(8,128)(2,1)} %bitcast.299), channel_id=1, replica_groups=mesh['section'=2,'dp'=16,'tensor'=4] {'tensor'}, dimensions={1} | all-to-all | bytes 1772544 | tf_op jit(solution)/shard_map/all_to_all | solution.py:43
  304.0 11.8 %all_gather.42 = bf16[577,768]{0,1:T(8,128)(2,1)S(1)} all-gather(bf16[577,192]{0,1:T(8,128)(2,1)} %reduce_sum.669), channel_id=1, replica_groups=mesh['section'=2,'dp'=16,'tensor'=4] {'tensor'}, dimensions={1}, use_global_device_ids=true | all-gather | bytes 1107840 | tf_op jit(solution)/shard_map/all_gather | solution.py:51
  333.0 19.0 %all_to_all.174 = bf16[577,4,192]{0,2,1:T(8,128)(2,1)} all-to-all(bf16[577,4,192]{0,2,1:T(8,128)(2,1)} %bitcast.300), channel_id=1, replica_groups=mesh['section'=2,'dp'=16,'tensor'=4] {'tensor'}, dimensions={1} | all-to-all | bytes 1772544 | tf_op jit(solution)/shard_map/all_to_all | solution.py:43
  353.4 11.3 %all_gather.43 = bf16[577,768]{0,1:T(8,128)(2,1)S(1)} all-gather(bf16[577,192]{0,1:T(8,128)(2,1)S(1)} %reduce_sum.673), channel_id=1, replica_groups=mesh['section'=2,'dp'=16,'tensor'=4] {'tensor'}, dimensions={1}, use_global_device_ids=true | all-gather | bytes 1107840 | tf_op jit(solution)/shard_map/all_gather | solution.py:51
  386.4 12.4 %all-to-all-done.9 = bf16[4,577,192]{1,2,0:T(8,128)(2,1)} async-done(((bf16[4,577,192]{1,2,0:T(8,128)(2,1)}), bf16[4,577,192]{1,2,0:T(8,128)(2,1)}, u32[]{:S(2)}, u32[]{:S(2)}) %all-to-all-start.9) | async-done | bytes 886304 | tf_op jit(solution)/shard_map/all_to_all | solution.py:183
  430.4 11.5 %all_gather.44 = bf16[577,768]{0,1:T(8,128)(2,1)S(1)} all-gather(bf16[577,192]{0,1:T(8,128)(2,1)} %reduce_sum.676), channel_id=1, replica_groups=mesh['section'=2,'dp'=16,'tensor'=4] {'tensor'}, dimensions={1}, use_global_device_ids=true | all-gather | bytes 1107840 | tf_op jit(solution)/shard_map/all_gather | solution.py:51
  478.7 11.3 %all_gather.45 = bf16[577,768]{0,1:T(8,128)(2,1)S(1)} all-gather(bf16[577,192]{0,1:T(8,128)(2,1)S(1)} %reduce_sum.680), channel_id=1, replica_groups=mesh['section'=2,'dp'=16,'tensor'=4] {'tensor'}, dimensions={1}, use_global_device_ids=true | all-gather | bytes 1107840 | tf_op jit(solution)/shard_map/all_gather | solution.py:51
  515.6 8.1 all-to-all-done.12
  556.5 11.9 %all_gather.46 = bf16[577,768]{0,1:T(8,128)(2,1)S(1)} all-gather(bf16[577,192]{0,1:T(8,128)(2,1)} %reduce_sum.683), channel_id=1, replica_groups=mesh['section'=2,'dp'=16,'tensor'=4] {'tensor'}, dimensions={1}, use_global_device_ids=true | all-gather | bytes 1107840 | tf_op jit(solution)/shard_map/all_gather | solution.py:51
  610.0 11.8 %all_gather.47 = bf16[577,768]{0,1:T(8,128)(2,1)S(1)} all-gather(bf16[577,192]{0,1:T(8,128)(2,1)S(1)} %reduce_sum.687), channel_id=1, replica_groups=mesh['section'=2,'dp'=16,'tensor'=4] {'tensor'}, dimensions={1}, use_global_device_ids=true | all-gather | bytes 1107840 | tf_op jit(solution)/shard_map/all_gather | solution.py:51
  625.1 62.2 %concatenate.3 = f32[1771776]{0:T(1024)} concatenate(f32[192]{0:T(256)S(1)} %add_add_fusion.9, f32[192]{0:T(256)S(1)} %add_add_fusion.8, f32[442368]{0:T(1024)S(1)} %copy-done.28, f32[384]{0:T(512)S(1)} %add.509, f32[147456]{0:T(1024)} %reshape.495, f32[192]{0:T(256)S(1)} %add_add_fusion.7, f32[192]{0:T(256)S(1)} %add_add_fusion.6, f32[192]{0:T(256)S(1)} %add_add_fusion.5, ...), dimensions={0} | concatenate | bytes 14174208 | tf_op jit(solution)/shard_map/concatenate | solution.py:380
  698.4 12.4 %all-to-all-done.5 = bf16[577,4,192]{0,2,1:T(8,128)(2,1)S(1)} async-done(((bf16[577,4,192]{0,2,1:T(8,128)(2,1)}), bf16[577,4,192]{0,2,1:T(8,128)(2,1)S(1)}, u32[]{:S(2)}, u32[]{:S(2)}) %all-to-all-start.5) | async-done | bytes 886304 | tf_op jit(solution)/shard_map/all_to_all | solution.py:43
  714.7 102.6 %all-reduce.2.cloned.1.call-done = f32[1771776]{0:T(1024)} async-done(((f32[1771776]{0:T(1024)}), f32[1771776]{0:T(1024)}) %all-reduce.2.cloned.1.call-update) | async-done | bytes 7087120 | tf_op jit(solution)/shard_map/psum | solution.py:37
  (490 shorter events, 371.4 us)
Async XLA Ops:
  7.2 59.9 %copy-start = (bf16[1,768,768]{2,1,0:T(8,128)(2,1)S(1)}, bf16[1,768,768]{2,1,0:T(8,128)(2,1)}, u32[]{:S(2)}) copy-start(bf16[1,768,768]{2,1,0:T(8,128)(2,1)} %param.25) | copy-start | bytes 3538948
  25.1 40.0 %copy-start.4 = (bf16[1,577,768]{1,2,0:T(8,128)(2,1)}, bf16[1,577,768]{1,2,0:T(8,128)(2,1)S(1)}, u32[]{:S(2)}) copy-start(bf16[1,577,768]{1,2,0:T(8,128)(2,1)S(1)} %all-gather) | copy-start | bytes 2658820
  34.1 18.4 %all-to-all-start = ((bf16[577,4,192]{0,2,1:T(8,128)(2,1)}), bf16[577,4,192]{0,2,1:T(8,128)(2,1)S(1)}, u32[]{:S(2)}, u32[]{:S(2)}) async-start(bf16[577,4,192]{0,2,1:T(8,128)(2,1)} %bitcast.12), calls=%async_computation | async-start | bytes 1966080 | tf_op jit(solution)/shard_map/all_to_all | solution.py:43
  38.2 360.6 %copy-start.93 = (f32[768]{0:T(1024)}, f32[768]{0:T(1024)S(1)}, u32[]{:S(2)}) copy-start(f32[768]{0:T(1024)S(1)} %reduce.44) | copy-start | bytes 9220
  75.8 18.0 %all-to-all-start.1 = ((bf16[577,4,192]{0,2,1:T(8,128)(2,1)}), bf16[577,4,192]{0,2,1:T(8,128)(2,1)S(1)}, u32[]{:S(2)}, u32[]{:S(2)}) async-start(bf16[577,4,192]{0,2,1:T(8,128)(2,1)} %bitcast.15), calls=%async_computation.1 | async-start | bytes 1966080 | tf_op jit(solution)/shard_map/all_to_all | solution.py:43
  95.1 20.0 %copy-start.68 = (bf16[577,192]{0,1:T(8,128)(2,1)}, bf16[577,192]{0,1:T(8,128)(2,1)S(1)}, u32[]{:S(2)}) copy-start(bf16[577,192]{0,1:T(8,128)(2,1)S(1)} %add_convert_fusion.15) | copy-start | bytes 664708
  95.2 7.0 collective-permute-start
  186.2 8.6 %collective-permute-start.1 = (bf16[577,192]{0,1:T(8,128)(2,1)S(1)}, bf16[577,192]{0,1:T(8,128)(2,1)S(1)}, u32[]{:S(2)}, u32[]{:S(2)}) collective-permute-start(bf16[577,192]{0,1:T(8,128)(2,1)S(1)} %add_convert_fusion.12), channel_id=1, source_target_pairs={{0,64},{1,65},{2,66},{3,67},{4,68},{5,69},{6,70},{7,71},{8,72},{9,... | collective-permute-start | bytes 664712 | tf_op jit(solution)/shard_map/ppermute | solution.py:14
  217.4 18.9 %all-to-all-start.4 = ((bf16[577,4,192]{0,2,1:T(8,128)(2,1)}), bf16[577,4,192]{0,2,1:T(8,128)(2,1)}, u32[]{:S(2)}, u32[]{:S(2)}) async-start(bf16[577,4,192]{0,2,1:T(8,128)(2,1)} %bitcast.295), calls=%async_computation.4 | async-start | bytes 1966080 | tf_op jit(solution)/shard_map/all_to_all | solution.py:43
  237.3 35.8 %all-to-all-start.6 = ((bf16[4,577,192]{1,2,0:T(8,128)(2,1)}), bf16[4,577,192]{1,2,0:T(8,128)(2,1)}, u32[]{:S(2)}, u32[]{:S(2)}) async-start(bf16[4,577,192]{1,2,0:T(8,128)(2,1)} %stack.60), calls=%async_computation.6 | async-start | bytes 1966080 | tf_op jit(solution)/shard_map/all_to_all | solution.py:183
  282.8 40.2 %slice-start.4 = ((s8[4485120]{0:T(1024)(128)(4,1)}), s8[290816]{0:T(1024)(128)(4,1)S(1)}, s32[]{:S(2)}) async-start(s8[4485120]{0:T(1024)(128)(4,1)} %bitcast.279), calls=%async_computation.20 | async-start | bytes 581632
  367.5 9.6 %collective-permute-start.2 = (bf16[577,192]{0,1:T(8,128)(2,1)S(1)}, bf16[577,192]{0,1:T(8,128)(2,1)}, u32[]{:S(2)}, u32[]{:S(2)}) collective-permute-start(bf16[577,192]{0,1:T(8,128)(2,1)S(1)} %get-tuple-element.62), channel_id=1, source_target_pairs={{64,0},{65,1},{66,2},{67,3},{68,4},{69,5},{70,6},{71,7},{72,8},{73... | collective-permute-start | bytes 664712 | tf_op jit(solution)/shard_map/ppermute | solution.py:14
  379.2 19.5 %all-to-all-start.9 = ((bf16[4,577,192]{1,2,0:T(8,128)(2,1)}), bf16[4,577,192]{1,2,0:T(8,128)(2,1)}, u32[]{:S(2)}, u32[]{:S(2)}) async-start(bf16[4,577,192]{1,2,0:T(8,128)(2,1)} %stack.62), calls=%async_computation.9 | async-start | bytes 1966080 | tf_op jit(solution)/shard_map/all_to_all | solution.py:183
  408.5 19.8 %all-to-all-start.10 = ((bf16[577,4,192]{0,2,1:T(8,128)(2,1)}), bf16[577,4,192]{0,2,1:T(8,128)(2,1)}, u32[]{:S(2)}, u32[]{:S(2)}) async-start(bf16[577,4,192]{0,2,1:T(8,128)(2,1)} %bitcast.296), calls=%async_computation.10 | async-start | bytes 1966080 | tf_op jit(solution)/shard_map/all_to_all | solution.py:43
  420.7 27.3 %slice-start.2 = ((s8[4485120]{0:T(1024)(128)(4,1)}), s8[290816]{0:T(1024)(128)(4,1)S(1)}, s32[]{:S(2)}) async-start(s8[4485120]{0:T(1024)(128)(4,1)} %bitcast.277), calls=%async_computation.18 | async-start | bytes 581632
  458.0 19.2 %all-to-all-start.11 = ((bf16[577,4,192]{0,2,1:T(8,128)(2,1)}), bf16[577,4,192]{0,2,1:T(8,128)(2,1)}, u32[]{:S(2)}, u32[]{:S(2)}) async-start(bf16[577,4,192]{0,2,1:T(8,128)(2,1)} %bitcast.294), calls=%async_computation.11 | async-start | bytes 1966080 | tf_op jit(solution)/shard_map/all_to_all | solution.py:43
  492.8 9.3 %collective-permute-start.3 = (bf16[577,192]{0,1:T(8,128)(2,1)S(1)}, bf16[577,192]{0,1:T(8,128)(2,1)S(1)}, u32[]{:S(2)}, u32[]{:S(2)}) collective-permute-start(bf16[577,192]{0,1:T(8,128)(2,1)S(1)} %get-tuple-element.60), channel_id=1, source_target_pairs={{64,0},{65,1},{66,2},{67,3},{68,4},{69,5},{70,6},{71,7},{72,8},{73... | collective-permute-start | bytes 664712 | tf_op jit(solution)/shard_map/ppermute | solution.py:14
  504.1 19.7 %all-to-all-start.12 = ((bf16[4,577,192]{1,2,0:T(8,128)(2,1)}), bf16[4,577,192]{1,2,0:T(8,128)(2,1)}, u32[]{:S(2)}, u32[]{:S(2)}) async-start(bf16[4,577,192]{1,2,0:T(8,128)(2,1)} %stack.64), calls=%async_computation.12 | async-start | bytes 1966080 | tf_op jit(solution)/shard_map/all_to_all | solution.py:183
  531.0 24.5 %all-to-all-start.13 = ((bf16[577,4,192]{0,2,1:T(8,128)(2,1)}), bf16[577,4,192]{0,2,1:T(8,128)(2,1)S(1)}, u32[]{:S(2)}, u32[]{:S(2)}) async-start(bf16[577,4,192]{0,2,1:T(8,128)(2,1)} %bitcast.71), calls=%async_computation.13 | async-start | bytes 1966080 | tf_op jit(solution)/shard_map/all_to_all | solution.py:43
  550.6 23.9 %slice-start = ((s8[4485120]{0:T(1024)(128)(4,1)}), s8[290816]{0:T(1024)(128)(4,1)S(1)}, s32[]{:S(2)}) async-start(s8[4485120]{0:T(1024)(128)(4,1)} %bitcast.275), calls=%async_computation.16 | async-start | bytes 581632
  584.8 23.7 %all-to-all-start.14 = ((bf16[577,4,192]{0,2,1:T(8,128)(2,1)}), bf16[577,4,192]{0,2,1:T(8,128)(2,1)}, u32[]{:S(2)}, u32[]{:S(2)}) async-start(bf16[577,4,192]{0,2,1:T(8,128)(2,1)} %bitcast.293), calls=%async_computation.14 | async-start | bytes 1966080 | tf_op jit(solution)/shard_map/all_to_all | solution.py:43
  589.2 228.2 %all-reduce.2.cloned.1.call-start = ((), (), s32[]{:S(2)}) async-start(), calls=%async_computation.15 | async-start | bytes 14180352 | tf_op jit(solution)/shard_map/psum | solution.py:37
  691.9 20.2 %copy-start.69 = (bf16[577,192]{0,1:T(8,128)(2,1)S(1)}, bf16[577,192]{0,1:T(8,128)(2,1)}, u32[]{:S(2)}) copy-start(bf16[577,192]{0,1:T(8,128)(2,1)} %copy-done.68) | copy-start | bytes 664708
  691.9 18.9 %all-to-all-start.5 = ((bf16[577,4,192]{0,2,1:T(8,128)(2,1)}), bf16[577,4,192]{0,2,1:T(8,128)(2,1)S(1)}, u32[]{:S(2)}, u32[]{:S(2)}) async-start(bf16[577,4,192]{0,2,1:T(8,128)(2,1)} %bitcast.38), calls=%async_computation.5 | async-start | bytes 1966080 | tf_op jit(solution)/shard_map/all_to_all | solution.py:43
  (116 other events, 411.6 us)
Sparse Core Ops, SparseCore 0:
  687.5 129.8 all-reduce.1
